TPU v7x, 32 devices: a whole 2x2x4 slice. The times are simulated.
32 devices in a mesh: grp: 8 (over z, core), own: 4 (over y, x).
Axes of the slice: x: 2, y: 2, z: 4, core: 2. Of those that a mesh axis runs over, the one named last changes fastest.
Arguments:
- tokens: bfloat16 [8192, 1024], P(('grp', 'own')), may hold values from -6 to 6
- cotangent: bfloat16 [8192, 1024], P(('grp', 'own')), may hold values from -6 to 6
- doc_lengths: int32 [4, 4], replicated, may hold values from 256 to 1280, as said below
- w_in: float32 [1024, 3072], P('own', 'grp'), may hold values from -0.1875 to 0.1875
- w_out: float32 [1024, 1024], P('own', 'grp'), may hold values from -0.1875 to 0.1875
- w_gate: float32 [1024, 4608], P('own', 'grp'), may hold values from -0.1875 to 0.1875
- w_up: float32 [1024, 4608], P('own', 'grp'), may hold values from -0.1875 to 0.1875
- w_down: float32 [4608, 1024], P('own', 'grp'), may hold values from -0.09375 to 0.09375
- conv_w: float32 [3, 1024], P(None, 'own'), may hold values from -3.5 to 3.5
- gain: float32 [1024], P('own'), may hold values from 0.5 to 1.5
- gain_two: float32 [1024], P('own'), may hold values from 0.5 to 1.5
- moment_in: float32 [1024, 3072], P('own', 'grp'), as said below
- moment_out: float32 [1024, 1024], P('own', 'grp'), as said below
- moment_gate: float32 [1024, 4608], P('own', 'grp'), as said below
- moment_up: float32 [1024, 4608], P('own', 'grp'), as said below
- moment_down: float32 [4608, 1024], P('own', 'grp'), as said below
- moment_conv: float32 [3, 1024], P(None, 'own'), as said below
- moment_gain: float32 [1024], P('own'), as said below
- moment_gain_two: float32 [1024], P('own'), as said below
- square_in: float32 [1024, 3072], P('own', 'grp'), as said below
- square_out: float32 [1024, 1024], P('own', 'grp'), as said below
- square_gate: float32 [1024, 4608], P('own', 'grp'), as said below
- square_up: float32 [1024, 4608], P('own', 'grp'), as said below
- square_down: float32 [4608, 1024], P('own', 'grp'), as said below
- square_conv: float32 [3, 1024], P(None, 'own'), as said below
- square_gain: float32 [1024], P('own'), as said below
- square_gain_two: float32 [1024], P('own'), as said below
Outputs:
- block_out: bfloat16 [8192, 1024], P(('grp', 'own'))
- grad_tokens: bfloat16 [8192, 1024], P(('grp', 'own'))
- grad_w_in: float32 [1024, 3072], P('own')
- grad_w_out: float32 [1024, 1024], P('own')
- grad_w_gate: float32 [1024, 4608], P('own')
- grad_w_up: float32 [1024, 4608], P('own')
- grad_w_down: float32 [4608, 1024], P('own')
- grad_conv_w: float32 [3, 1024], P(None, 'own')
- grad_gain: float32 [1024], P('own')
- grad_gain_two: float32 [1024], P('own')
- new_w_in: float32 [1024, 3072], P('own', 'grp')
- new_w_out: float32 [1024, 1024], P('own', 'grp')
- new_w_gate: float32 [1024, 4608], P('own', 'grp')
- new_w_up: float32 [1024, 4608], P('own', 'grp')
- new_w_down: float32 [4608, 1024], P('own', 'grp')
- new_conv_w: float32 [3, 1024], P(None, 'own')
- new_gain: float32 [1024], P('own')
- new_gain_two: float32 [1024], P('own')
- new_moment_in: float32 [1024, 3072], P('own', 'grp')
- new_moment_out: float32 [1024, 1024], P('own', 'grp')
- new_moment_gate: float32 [1024, 4608], P('own', 'grp')
- new_moment_up: float32 [1024, 4608], P('own', 'grp')
- new_moment_down: float32 [4608, 1024], P('own', 'grp')
- new_moment_conv: float32 [3, 1024], P(None, 'own')
- new_moment_gain: float32 [1024], P('own')
- new_moment_gain_two: float32 [1024], P('own')
- new_square_in: float32 [1024, 3072], P('own', 'grp')
- new_square_out: float32 [1024, 1024], P('own', 'grp')
- new_square_gate: float32 [1024, 4608], P('own', 'grp')
- new_square_up: float32 [1024, 4608], P('own', 'grp')
- new_square_down: float32 [4608, 1024], P('own', 'grp')
- new_square_conv: float32 [3, 1024], P(None, 'own')
- new_square_gain: float32 [1024], P('own')
- new_square_gain_two: float32 [1024], P('own')
Inputs may be any that keep to these rules, and one draw needn't show every extreme that they name: `doc_lengths`: the 4 lengths of each sequence sum to 2048. `moment_in`: first moments: real values of either sign. `moment_out`: first moments: real values of either sign. `moment_gate`: first moments: real values of either sign. `moment_up`: first moments: real values of either sign. `moment_down`: first moments: real values of either sign. `moment_conv`: first moments: real values of either sign. `moment_gain`: first moments: real values of either sign. `moment_gain_two`: first moments: real values of either sign. `square_in`: second moments are positive. `square_out`: second moments are positive. `square_gate`: second moments are positive. `square_up`: second moments are positive. `square_down`: second moments are positive. `square_conv`: second moments are positive. `square_gain`: second moments are positive. `square_gain_two`: second moments are positive.
All inputs are finite; a program needn't handle non-finite values.
Results may differ from a plain program's by a relative error of at most 0.025.
Values may be sent and summed in bfloat16 or wider, within the bound.
No kernel may reach another device: no remote copies, remote signals or barrier semaphores. Data moves between devices by JAX's collectives and lax.ppermute only.
A program may use at most 320 MiB of HBM per device.

v0:
```python
import jax
import jax.numpy as jnp
from jax import lax
from jax.sharding import PartitionSpec as P

SEQ_LEN = 2048
eps_norm = 1e-05
eps_adam = 1e-08
beta_one = 0.9
beta_two = 0.95
train_step = 5
rate_matrix = 0.004
rate_vector = 0.1
decay_matrix = 0.1


def passed_along(block, axis, distance):
    devices = range(lax.axis_size(axis))
    route = [(i - distance, i) for i in devices if i - distance in devices]
    return lax.ppermute(block, axis, route)


def stream_starts(doc_lengths, seq_len):
    starts = jnp.cumsum(doc_lengths, axis=1) - doc_lengths
    base = (jnp.arange(doc_lengths.shape[0], dtype=jnp.int32) * seq_len)[:, None]
    first = (jnp.arange(doc_lengths.shape[1], dtype=jnp.int32) == 0)[None, :]
    return jnp.where(first, 0, base + starts).reshape(-1)


def since_start(positions, stream):
    below = jnp.where(stream[None, :] <= positions[:, None], stream[None, :], 0)
    return positions - jnp.max(below, axis=1)


def apply_adam(param, first, second, grad, rate, decay):
    first_new = beta_one * first + (1.0 - beta_one) * grad
    second_new = beta_two * second + (1.0 - beta_two) * grad * grad
    first_hat = first_new / (1.0 - beta_one**train_step)
    second_hat = second_new / (1.0 - beta_two**train_step)
    param_new = param - rate * (first_hat / (jnp.sqrt(second_hat) + eps_adam) + decay * param)
    return (param_new, first_new, second_new)


def local(
    tokens,
    cotangent,
    doc_lengths,
    w_in,
    w_out,
    w_gate,
    w_up,
    w_down,
    conv_w,
    gain,
    gain_two,
    moment_in,
    moment_out,
    moment_gate,
    moment_up,
    moment_down,
    moment_conv,
    moment_gain,
    moment_gain_two,
    square_in,
    square_out,
    square_gate,
    square_up,
    square_down,
    square_conv,
    square_gain,
    square_gain_two,
):
    across = (
        lax.all_gather(w_in.astype(jnp.bfloat16), "grp", axis=1, tiled=True),
        lax.all_gather(w_out.astype(jnp.bfloat16), "grp", axis=1, tiled=True),
        lax.all_gather(w_gate.astype(jnp.bfloat16), "grp", axis=1, tiled=True),
        lax.all_gather(w_up.astype(jnp.bfloat16), "grp", axis=1, tiled=True),
        lax.all_gather(w_down.astype(jnp.bfloat16), "grp", axis=1, tiled=True),
    )
    in_half, out_half, gate_half, up_half, down_half, conv_half, gain_half, gain_two_half = (
        lax.all_gather(across[0], "own", axis=0, tiled=True),
        lax.all_gather(across[1], "own", axis=0, tiled=True),
        lax.all_gather(across[2], "own", axis=0, tiled=True),
        lax.all_gather(across[3], "own", axis=0, tiled=True),
        lax.all_gather(across[4], "own", axis=0, tiled=True),
        lax.all_gather(conv_w.astype(jnp.bfloat16), "own", axis=1, tiled=True),
        lax.all_gather(gain.astype(jnp.bfloat16), "own", axis=0, tiled=True),
        lax.all_gather(gain_two.astype(jnp.bfloat16), "own", axis=0, tiled=True),
    )
    conv_float = conv_half.astype(jnp.float32)
    gain_float = gain_half.astype(jnp.float32)
    gain_two_float = gain_two_half.astype(jnp.float32)
    rows, width = tokens.shape
    hidden_width = gate_half.shape[1]
    taps = conv_half.shape[0]
    device = lax.axis_index(("grp", "own"))
    first_row = device * rows
    stream = stream_starts(doc_lengths, SEQ_LEN)
    position = first_row + jnp.arange(rows + taps - 1, dtype=jnp.int32)
    since = since_start(position, stream)
    x_float = tokens.astype(jnp.float32)
    cot_float = cotangent.astype(jnp.float32)
    inv_rms = lax.rsqrt(jnp.mean(x_float * x_float, axis=1, keepdims=True) + eps_norm)
    normed = (x_float * inv_rms * gain_float).astype(jnp.bfloat16)
    project = jnp.dot(normed, in_half, preferred_element_type=jnp.float32)
    b_gate = project[:, :width]
    c_gate = project[:, width : 2 * width]
    x_value = project[:, 2 * width :]
    gated = b_gate * x_value
    before = passed_along(gated[rows - taps + 1 :], ("grp", "own"), 1)
    extended = jnp.concatenate([before, gated], 0)
    convolved = jnp.zeros((rows, width), jnp.float32)
    for tap_index in range(taps):
        keep = (since[:rows] >= tap_index)[:, None]
        moved = extended[taps - 1 - tap_index : taps - 1 - tap_index + rows]
        convolved = convolved + jnp.where(keep, conv_float[tap_index] * moved, 0.0)
    mixed = (c_gate * convolved).astype(jnp.bfloat16)
    middle = x_float + jnp.dot(mixed, out_half, preferred_element_type=jnp.float32)
    inv_two = lax.rsqrt(jnp.mean(middle * middle, axis=1, keepdims=True) + eps_norm)
    normed_two = (middle * inv_two * gain_two_float).astype(jnp.bfloat16)
    gate = jnp.dot(normed_two, gate_half, preferred_element_type=jnp.float32)
    up = jnp.dot(normed_two, up_half, preferred_element_type=jnp.float32)
    sig = jax.nn.sigmoid(gate)
    activated = gate * sig
    hidden = (activated * up).astype(jnp.bfloat16)
    block_out = (middle + jnp.dot(hidden, down_half, preferred_element_type=jnp.float32)).astype(
        jnp.bfloat16
    )
    grad_hidden = jnp.dot(cotangent, down_half.T, preferred_element_type=jnp.float32)
    grad_gate = (grad_hidden * up * sig * (1.0 + gate * (1.0 - sig))).astype(jnp.bfloat16)
    grad_up = (grad_hidden * activated).astype(jnp.bfloat16)
    grad_normed_two = jnp.dot(grad_gate, gate_half.T, preferred_element_type=jnp.float32) + jnp.dot(
        grad_up, up_half.T, preferred_element_type=jnp.float32
    )
    gain_two_rows = jnp.sum(grad_normed_two * middle * inv_two, axis=0)
    weighted_two = gain_two_float * grad_normed_two
    grad_middle = (
        cot_float
        + inv_two * weighted_two
        - middle
        * inv_two
        * inv_two
        * inv_two
        * jnp.mean(weighted_two * middle, axis=1, keepdims=True)
    )
    grad_middle_half = grad_middle.astype(jnp.bfloat16)
    grad_mixed = jnp.dot(grad_middle_half, out_half.T, preferred_element_type=jnp.float32)
    grad_c = grad_mixed * convolved
    grad_conv = grad_mixed * c_gate
    after = passed_along(grad_conv[: taps - 1], ("grp", "own"), -1)
    grad_extended = jnp.concatenate([grad_conv, after], 0)
    grad_gated = jnp.zeros((rows, width), jnp.float32)
    tap_sums = []
    for tap_index in range(taps):
        keep_ahead = (since[tap_index : tap_index + rows] >= tap_index)[:, None]
        grad_gated = grad_gated + conv_float[tap_index] * jnp.where(
            keep_ahead, grad_extended[tap_index : tap_index + rows], 0.0
        )
        keep = (since[:rows] >= tap_index)[:, None]
        moved = extended[taps - 1 - tap_index : taps - 1 - tap_index + rows]
        tap_sums.append(jnp.sum(jnp.where(keep, grad_conv * moved, 0.0), axis=0))
    grad_b = grad_gated * x_value
    grad_x = grad_gated * b_gate
    grad_project = jnp.concatenate([grad_b, grad_c, grad_x], 1).astype(jnp.bfloat16)
    grad_normed = jnp.dot(grad_project, in_half.T, preferred_element_type=jnp.float32)
    gain_rows = jnp.sum(grad_normed * x_float * inv_rms, axis=0)
    weighted = gain_float * grad_normed
    grad_tokens = (
        grad_middle
        + inv_rms * weighted
        - x_float
        * inv_rms
        * inv_rms
        * inv_rms
        * jnp.mean(weighted * x_float, axis=1, keepdims=True)
    ).astype(jnp.bfloat16)
    small_terms = jnp.stack(tap_sums + [gain_rows, gain_two_rows], axis=1)
    wide_terms = jnp.concatenate(
        [
            jnp.dot(normed.T, grad_project, preferred_element_type=jnp.float32),
            jnp.dot(mixed.T, grad_middle_half, preferred_element_type=jnp.float32),
            jnp.dot(normed_two.T, grad_gate, preferred_element_type=jnp.float32),
            jnp.dot(normed_two.T, grad_up, preferred_element_type=jnp.float32),
        ],
        1,
    )
    down_terms = jnp.dot(hidden.T, cotangent, preferred_element_type=jnp.float32)
    shares = (
        lax.psum_scatter(
            wide_terms.astype(jnp.bfloat16), "own", scatter_dimension=0, tiled=True
        ).astype(jnp.float32),
        lax.psum_scatter(
            down_terms.astype(jnp.bfloat16), "own", scatter_dimension=0, tiled=True
        ).astype(jnp.float32),
        lax.psum_scatter(
            small_terms.astype(jnp.bfloat16), "own", scatter_dimension=0, tiled=True
        ).astype(jnp.float32),
    )
    wide_share, down_share, small_share = (
        lax.psum(shares[0].astype(jnp.bfloat16), "grp").astype(jnp.float32),
        lax.psum(shares[1].astype(jnp.bfloat16), "grp").astype(jnp.float32),
        lax.psum(shares[2].astype(jnp.bfloat16), "grp").astype(jnp.float32),
    )
    grad_w_in = wide_share[:, : 3 * width]
    grad_w_out = wide_share[:, 3 * width : 4 * width]
    grad_w_gate = wide_share[:, 4 * width : 4 * width + hidden_width]
    grad_w_up = wide_share[:, 4 * width + hidden_width :]
    grad_conv_w = small_share[:, :taps].T
    grad_gain = small_share[:, taps]
    grad_gain_two = small_share[:, taps + 1]
    column = lax.axis_index("grp")

    def own_columns(grad, param):
        count = param.shape[1]
        return lax.dynamic_slice_in_dim(grad, column * count, count, 1)

    new_w_in, new_moment_in, new_square_in = apply_adam(
        w_in, moment_in, square_in, own_columns(grad_w_in, w_in), rate_matrix, decay_matrix
    )
    new_w_out, new_moment_out, new_square_out = apply_adam(
        w_out, moment_out, square_out, own_columns(grad_w_out, w_out), rate_matrix, decay_matrix
    )
    new_w_gate, new_moment_gate, new_square_gate = apply_adam(
        w_gate,
        moment_gate,
        square_gate,
        own_columns(grad_w_gate, w_gate),
        rate_matrix,
        decay_matrix,
    )
    new_w_up, new_moment_up, new_square_up = apply_adam(
        w_up, moment_up, square_up, own_columns(grad_w_up, w_up), rate_matrix, decay_matrix
    )
    new_w_down, new_moment_down, new_square_down = apply_adam(
        w_down, moment_down, square_down, own_columns(down_share, w_down), rate_matrix, decay_matrix
    )
    new_conv_w, new_moment_conv, new_square_conv = apply_adam(
        conv_w, moment_conv, square_conv, grad_conv_w, rate_vector, 0.0
    )
    new_gain, new_moment_gain, new_square_gain = apply_adam(
        gain, moment_gain, square_gain, grad_gain, rate_vector, 0.0
    )
    new_gain_two, new_moment_gain_two, new_square_gain_two = apply_adam(
        gain_two, moment_gain_two, square_gain_two, grad_gain_two, rate_vector, 0.0
    )
    return (
        block_out,
        grad_tokens,
        grad_w_in,
        grad_w_out,
        grad_w_gate,
        grad_w_up,
        down_share,
        grad_conv_w,
        grad_gain,
        grad_gain_two,
        new_w_in,
        new_w_out,
        new_w_gate,
        new_w_up,
        new_w_down,
        new_conv_w,
        new_gain,
        new_gain_two,
        new_moment_in,
        new_moment_out,
        new_moment_gate,
        new_moment_up,
        new_moment_down,
        new_moment_conv,
        new_moment_gain,
        new_moment_gain_two,
        new_square_in,
        new_square_out,
        new_square_gate,
        new_square_up,
        new_square_down,
        new_square_conv,
        new_square_gain,
        new_square_gain_two,
    )


def solution(mesh):
    placed = (
        P(("grp", "own"), None),
        P(("grp", "own"), None),
        P(),
        P("own", "grp"),
        P("own", "grp"),
        P("own", "grp"),
        P("own", "grp"),
        P("own", "grp"),
        P(None, "own"),
        P("own"),
        P("own"),
        P("own", "grp"),
        P("own", "grp"),
        P("own", "grp"),
        P("own", "grp"),
        P("own", "grp"),
        P(None, "own"),
        P("own"),
        P("own"),
        P("own", "grp"),
        P("own", "grp"),
        P("own", "grp"),
        P("own", "grp"),
        P("own", "grp"),
        P(None, "own"),
        P("own"),
        P("own"),
    )
    return jax.shard_map(
        local,
        mesh=mesh,
        in_specs=placed,
        out_specs=(
            P(("grp", "own"), None),
            P(("grp", "own"), None),
            P("own", None),
            P("own", None),
            P("own", None),
            P("own", None),
            P("own", None),
            P(None, "own"),
            P("own"),
            P("own"),
            P("own", "grp"),
            P("own", "grp"),
            P("own", "grp"),
            P("own", "grp"),
            P("own", "grp"),
            P(None, "own"),
            P("own"),
            P("own"),
            P("own", "grp"),
            P("own", "grp"),
            P("own", "grp"),
            P("own", "grp"),
            P("own", "grp"),
            P(None, "own"),
            P("own"),
            P("own"),
            P("own", "grp"),
            P("own", "grp"),
            P("own", "grp"),
            P("own", "grp"),
            P("own", "grp"),
            P(None, "own"),
            P("own"),
            P("own"),
        ),
        check_vma=False,
    )
```

profile of v0, /device:TPU:0, one launch (start us, length us, event | category | flops | bytes accessed | tf_op | source)
XLA Modules:
  0.0 1173.6 jit_solution(15216509789549518167)
XLA Ops:
  7.3 1.7 convert_element_type.91
  9.1 1.8 convert_element_type.99
  11.0 1.8 convert_element_type.100
  12.8 1.8 convert_element_type.102
  14.7 23.3 %all-gather.12.cloned.1.call-done = bf16[256,3072]{1,0:T(8,128)(2,1)} async-done(((bf16[256,384]{1,0:T(8,128)(2,1)}), bf16[256,3072]{1,0:T(8,128)(2,1)}) %all-gather.12.cloned.1.call-update) | async-done | bytes 1572880 | tf_op jit(solution)/shard_map/all_gather | solution.py:74
  38.1 14.9 %all_gather.43 = bf16[256,1024]{1,0:T(8,128)(2,1)} all-gather(bf16[256,128]{1,0:T(8,128)(2,1)S(1)} %convert_element_type.95), channel_id=1, replica_groups=mesh['grp'=8,'own'=4] {'grp'}, dimensions={1}, use_global_device_ids=true | all-gather | bytes 589824 | tf_op jit(solution)/shard_map/all_gather | solution.py:75
  53.1 18.9 %all-gather.18.cloned.1.call-done = bf16[256,4608]{0,1:T(8,128)(2,1)} async-done(((bf16[256,576]{0,1:T(8,128)(2,1)}), bf16[256,4608]{0,1:T(8,128)(2,1)}) %all-gather.18.cloned.1.call-update) | async-done | bytes 2359312 | tf_op jit(solution)/shard_map/all_gather | solution.py:76
  72.1 32.5 %all-gather.22.cloned.1.call-done = bf16[256,4608]{0,1:T(8,128)(2,1)} async-done(((bf16[256,576]{0,1:T(8,128)(2,1)}), bf16[256,4608]{0,1:T(8,128)(2,1)}) %all-gather.22.cloned.1.call-update) | async-done | bytes 2359312 | tf_op jit(solution)/shard_map/all_gather | solution.py:77
  104.7 33.9 %all-gather.26.cloned.1.call-done = bf16[1152,1024]{1,0:T(8,128)(2,1)} async-done(((bf16[1152,128]{1,0:T(8,128)(2,1)}), bf16[1152,1024]{1,0:T(8,128)(2,1)}) %all-gather.26.cloned.1.call-update) | async-done | bytes 2359312 | tf_op jit(solution)/shard_map/all_gather | solution.py:78
  138.7 8.0 all-gather
  147.2 8.3 all_gather.42
  155.9 53.3 %all-gather.14.cloned.1.call-done = bf16[1024,3072]{1,0:T(8,128)(2,1)} async-done(((bf16[256,3072]{1,0:T(8,128)(2,1)}), bf16[1024,3072]{1,0:T(8,128)(2,1)}) %all-gather.14.cloned.1.call-update) | async-done | bytes 6291472 | tf_op jit(solution)/shard_map/all_gather | solution.py:81
  209.2 4.7 fusion.30
  214.0 3.4 collective-permute-start
  217.5 8.4 all-gather.1
  225.9 1.5 multiply_convert_fusion.7
  227.4 18.7 %all-gather.16.cloned.1.call-done = bf16[1024,1024]{1,0:T(8,128)(2,1)} async-done(((bf16[256,1024]{1,0:T(8,128)(2,1)}), bf16[1024,1024]{1,0:T(8,128)(2,1)}) %all-gather.16.cloned.1.call-update) | async-done | bytes 2097168 | tf_op jit(solution)/shard_map/all_gather | solution.py:82
  246.1 2.4 multiply_reduce_fusion.2
  248.7 95.3 %all-gather.20.cloned.1.call-done = bf16[1024,4608]{0,1:T(8,128)(2,1)} async-done(((bf16[256,4608]{0,1:T(8,128)(2,1)}), bf16[1024,4608]{0,1:T(8,128)(2,1)}) %all-gather.20.cloned.1.call-update) | async-done | bytes 9437200 | tf_op jit(solution)/shard_map/all_gather | solution.py:83
  344.0 11.5 fusion.51
  355.5 86.4 %all-gather.24.cloned.1.call-done = bf16[1024,4608]{0,1:T(8,128)(2,1)} async-done(((bf16[256,4608]{0,1:T(8,128)(2,1)}), bf16[1024,4608]{0,1:T(8,128)(2,1)}) %all-gather.24.cloned.1.call-update) | async-done | bytes 9437200 | tf_op jit(solution)/shard_map/all_gather | solution.py:84
  441.9 11.5 fusion.52
  453.5 86.5 %all-gather.28.cloned.1.call-done = bf16[4608,1024]{1,0:T(8,128)(2,1)} async-done(((bf16[1152,1024]{1,0:T(8,128)(2,1)}), bf16[4608,1024]{1,0:T(8,128)(2,1)}) %all-gather.28.cloned.1.call-update) | async-done | bytes 9437200 | tf_op jit(solution)/shard_map/all_gather | solution.py:85
  540.0 13.8 %multiply_convert_fusion = (bf16[256,4608]{1,0:T(8,128)(2,1)}, bf16[256,4608]{1,0:T(8,128)(2,1)}, bf16[256,4608]{1,0:T(8,128)(2,1)S(1)}) fusion(f32[256,4608]{1,0:T(8,128)} %fusion.51, f32[256,4608]{1,0:T(8,128)} %fusion.52, bf16[256,1024]{1,0:T(8,128)(2,1)S(1)} %copy-done.16, bf16[4608,1024]{1,0:T(8,128)(2,1)} %all-gather.28.cloned.1.call-done), kind=kOutput, calls=%fused_computation.5 | convolution fusion | flops 2433613824 | bytes 26476544 | tf_op jit(solution)/shard_map/dot_general | solution.py:129
  553.8 1.4 copy-done.11
  555.2 5.0 convolution_convert_fusion
  560.6 6.0 fusion.53
  566.6 5.9 multiply_reduce_fusion
  575.6 1.6 collective-permute-start.1
  577.2 5.1 convolution_convert_fusion.1
  582.3 5.2 convolution_convert_fusion.2
  587.6 2.1 convolution_convert_fusion.4
  591.0 4.5 convolution_convert_fusion.3
  595.6 31.4 %pad_maximum_fusion = bf16[1024,13312]{0,1:T(8,128)(2,1)} fusion(bf16[1024,4608]{0,1:T(8,128)(2,1)} %convolution_convert_fusion.1, bf16[1024,4608]{0,1:T(8,128)(2,1)} %convolution_convert_fusion.2, bf16[1024,1024]{0,1:T(8,128)(2,1)} %convolution_convert_fusion.4, bf16[1024,3072]{0,1:T(8,128)(2,1)} %convolution_convert_fusion.3), kind=kLoop, calls=%fused_computation | loop fusion | flops 109051904 | bytes 54525952 | tf_op jit(solution)/shard_map/concatenate | solution.py:178
  627.4 6.6 fusion.18
  634.8 20.7 %reduce-scatter.6.cloned.1.call-done = bf16[1152,1024]{1,0:T(8,128)(2,1)} async-done(((bf16[4608,1024]{1,0:T(8,128)(2,1)}), bf16[1152,1024]{1,0:T(8,128)(2,1)}) %reduce-scatter.6.cloned.1.call-update) | async-done | bytes 2359312 | tf_op jit(solution)/shard_map/reduce_scatter | solution.py:192
  655.5 241.9 %reduce-scatter.4.cloned.1.call-done = bf16[256,13312]{0,1:T(8,128)(2,1)} async-done(((bf16[1024,13312]{0,1:T(8,128)(2,1)}), bf16[256,13312]{0,1:T(8,128)(2,1)}) %reduce-scatter.4.cloned.1.call-update) | async-done | bytes 6815760 | tf_op jit(solution)/shard_map/reduce_scatter | solution.py:189
  899.0 1.9 copy.109
  900.9 1.9 copy.110
  902.8 1.7 copy.113
  904.5 1.7 copy.114
  906.2 7.9 fusion.1
  914.1 1.2 fusion.14
  915.3 8.1 reduce-scatter.8.cloned.1.call-done
  923.4 16.4 %psum.23 = bf16[256,5]{0,1:T(8,128)(2,1)S(1)} all-reduce(bf16[256,5]{0,1:T(8,128)(2,1)} %reduce-scatter.8.cloned.1.call-done), channel_id=1, replica_groups=mesh['grp'=8,'own'=4] {'grp'}, use_global_device_ids=true, to_apply=%region_16.17 | all-reduce | flops 1280 | bytes 5120 | tf_op jit(solution)/shard_map/psum | solution.py:202
  941.1 175.2 %all-reduce.3.cloned.1.call-done = (bf16[256,13312]{0,1:T(8,128)(2,1)}, bf16[1152,1024]{1,0:T(8,128)(2,1)}) async-done(((bf16[256,13312]{0,1:T(8,128)(2,1)}, bf16[1152,1024]{1,0:T(8,128)(2,1)}), (bf16[256,13312]{0,1:T(8,128)(2,1)}, bf16[1152,1024]{1,0:T(8,128)(2,1)})) %all-reduce.3.cloned.1.call-update) | async-done | bytes 9175056 | tf_op jit(solution)/shard_map/psum | solution.py:200
  1116.3 1.8 slice.111
  1118.2 2.4 slice.112
  1120.6 4.4 fusion.48
  1125.0 2.4 copy.117
  1127.3 2.5 copy.118
  1129.9 6.0 copy.119
  1135.9 6.0 copy.120
  1142.0 4.5 convert_element_type.111
  1146.4 1.2 multiply_subtract_fusion.4
  1147.6 2.1 copy.121
  1149.7 1.9 multiply_subtract_fusion.5
  1151.6 1.7 copy.122
  1153.2 1.9 copy.123
  1155.2 1.7 copy.124
  1156.8 1.9 copy.125
  1158.7 1.7 copy.126
  1160.4 3.1 multiply_subtract_fusion.1
  1163.5 3.6 multiply_subtract_fusion.2
  (159 shorter events, 10.4 us)
Async XLA Ops:
  7.2 30.9 %copy-start.26 = (f32[256,128]{1,0:T(8,128)S(1)}, f32[256,128]{1,0:T(8,128)}, u32[]{:S(2)}) copy-start(f32[256,128]{1,0:T(8,128)} %param.31) | copy-start | bytes 393220
  7.2 30.8 %all-gather.12.cloned.1.call-start = ((), (), s32[]{:S(2)}) async-start(), calls=%async_computation.3 | async-start | bytes 1769472 | tf_op jit(solution)/shard_map/all_gather | solution.py:74
  9.0 63.0 %all-gather.18.cloned.1.call-start = ((), (), s32[]{:S(2)}) async-start(), calls=%async_computation.6 | async-start | bytes 2654208 | tf_op jit(solution)/shard_map/all_gather | solution.py:76
  10.9 93.7 %all-gather.22.cloned.1.call-start = ((), (), s32[]{:S(2)}) async-start(), calls=%async_computation.8 | async-start | bytes 2654208 | tf_op jit(solution)/shard_map/all_gather | solution.py:77
  12.8 125.8 %all-gather.26.cloned.1.call-start = ((), (), s32[]{:S(2)}) async-start(), calls=%async_computation.10 | async-start | bytes 2654208 | tf_op jit(solution)/shard_map/all_gather | solution.py:78
  14.7 194.5 %all-gather.14.cloned.1.call-start = ((), (), s32[]{:S(2)}) async-start(), calls=%async_computation.4 | async-start | bytes 7864320 | tf_op jit(solution)/shard_map/all_gather | solution.py:81
  38.0 100.7 %copy-start.36 = (f32[256]{0:T(256)S(1)}, f32[256]{0:T(256)}, u32[]{:S(2)}) copy-start(f32[256]{0:T(256)} %param.36) | copy-start | bytes 3076
  38.0 108.8 %copy-start.30 = (f32[3,256]{1,0:T(4,128)S(1)}, f32[3,256]{1,0:T(4,128)}, u32[]{:S(2)}) copy-start(f32[3,256]{1,0:T(4,128)} %param.35) | copy-start | bytes 9220
  38.0 108.8 %copy-start.31 = (s32[4,4]{1,0:T(4,128)S(1)}, s32[4,4]{1,0:T(4,128)}, u32[]{:S(2)}) copy-start(s32[4,4]{1,0:T(4,128)} %param.29) | copy-start | bytes 196
  38.0 117.6 %copy-start.6 = (bf16[256,1024]{1,0:T(8,128)(2,1)S(1)}, bf16[256,1024]{1,0:T(8,128)(2,1)}, u32[]{:S(2)}) copy-start(bf16[256,1024]{1,0:T(8,128)(2,1)} %param.27) | copy-start | bytes 1572868
  38.1 208.0 %all-gather.16.cloned.1.call-start = ((), (), s32[]{:S(2)}) async-start(), calls=%async_computation.5 | async-start | bytes 2621440 | tf_op jit(solution)/shard_map/all_gather | solution.py:82
  53.0 291.0 %all-gather.20.cloned.1.call-start = ((), (), s32[]{:S(2)}) async-start(), calls=%async_computation.7 | async-start | bytes 11796480 | tf_op jit(solution)/shard_map/all_gather | solution.py:83
  72.1 369.9 %all-gather.24.cloned.1.call-start = ((), (), s32[]{:S(2)}) async-start(), calls=%async_computation.9 | async-start | bytes 11796480 | tf_op jit(solution)/shard_map/all_gather | solution.py:84
  104.7 435.4 %all-gather.28.cloned.1.call-start = ((), (), s32[]{:S(2)}) async-start(), calls=%async_computation.11 | async-start | bytes 11796480 | tf_op jit(solution)/shard_map/all_gather | solution.py:85
  138.7 516.8 %reduce-scatter.6.cloned.1.call-start = ((), (), s32[]{:S(2)}) async-start(), calls=%async_computation.13 | async-start | bytes 11796480 | tf_op jit(solution)/shard_map/reduce_scatter | solution.py:192
  209.2 8.3 copy-start.37
  213.8 12.0 %copy-start.1 = (f32[256,3072]{1,0:T(8,128)}, f32[256,3072]{1,0:T(8,128)S(1)}, u32[]{:S(2)}) copy-start(f32[256,3072]{1,0:T(8,128)S(1)} %fusion.30) | copy-start | bytes 9437188
  214.0 11.9 %collective-permute-start = (f32[2,1024]{1,0:T(2,128)S(1)}, f32[2,1024]{1,0:T(2,128)S(1)}, u32[]{:S(2)}, u32[]{:S(2)}) collective-permute-start(f32[2,1024]{1,0:T(2,128)S(1)} %slice.104), channel_id=1, source_target_pairs={{0,1},{1,2},{2,3},{3,4},{4,5},{5,6},{6,7},{7,8},{8,9},{9,10},{10,1... | collective-permute-start | bytes 24584 | tf_op jit(solution)/shard_map/ppermute | solution.py:20
  227.4 128.1 %copy-start.8 = (bf16[256,1024]{1,0:T(8,128)(2,1)}, bf16[256,1024]{1,0:T(8,128)(2,1)S(1)}, u32[]{:S(2)}) copy-start(bf16[256,1024]{1,0:T(8,128)(2,1)S(1)} %get-tuple-element.207) | copy-start | bytes 1572868
  248.7 193.3 %copy-start.4 = (bf16[256,1024]{1,0:T(8,128)(2,1)}, bf16[256,1024]{1,0:T(8,128)(2,1)S(1)}, u32[]{:S(2)}) copy-start(bf16[256,1024]{1,0:T(8,128)(2,1)S(1)} %multiply_convert_fusion.6) | copy-start | bytes 1572868
  441.9 98.1 %copy-start.16 = (bf16[256,1024]{1,0:T(8,128)(2,1)S(1)}, bf16[256,1024]{1,0:T(8,128)(2,1)}, u32[]{:S(2)}) copy-start(bf16[256,1024]{1,0:T(8,128)(2,1)} %param.28) | copy-start | bytes 1572868
  553.8 1.4 copy-start.11
  560.3 337.1 %reduce-scatter.4.cloned.1.call-start = ((), (), s32[]{:S(2)}) async-start(), calls=%async_computation.12 | async-start | bytes 34078720 | tf_op jit(solution)/shard_map/reduce_scatter | solution.py:189
  560.5 6.1 copy-start.15
  566.6 5.9 copy-start.17
  566.6 6.3 copy-start.3
  572.5 2.1 copy-start.2
  572.5 2.5 copy-start.10
  572.9 4.3 copy-start.5
  575.6 14.8 %copy-start.28 = (bf16[256,1024]{1,0:T(8,128)(2,1)}, bf16[256,1024]{1,0:T(8,128)(2,1)S(1)}, u32[]{:S(2)}) copy-start(bf16[256,1024]{1,0:T(8,128)(2,1)S(1)} %get-tuple-element.214) | copy-start | bytes 1572868
  575.6 6.7 copy-start.14
  575.6 14.0 %collective-permute-start.1 = (f32[2,1024]{1,0:T(2,128)S(1)}, f32[2,1024]{1,0:T(2,128)S(1)}, u32[]{:S(2)}, u32[]{:S(2)}) collective-permute-start(f32[2,1024]{1,0:T(2,128)S(1)} %slice.108), channel_id=1, source_target_pairs={{1,0},{2,1},{3,2},{4,3},{5,4},{6,5},{7,6},{8,7},{9,8},{10,9},{11,1... | collective-permute-start | bytes 24584 | tf_op jit(solution)/shard_map/ppermute | solution.py:20
  582.3 5.2 copy-start.9
  587.6 3.5 copy-start.7
  590.2 0.8 copy-start.29
  627.0 296.4 %reduce-scatter.8.cloned.1.call-start = ((), (), s32[]{:S(2)}) async-start(), calls=%async_computation.14 | async-start | bytes 20480 | tf_op jit(solution)/shard_map/reduce_scatter | solution.py:195
  634.0 263.4 %copy-start.18 = (f32[256,384]{1,0:T(8,128)S(1)}, f32[256,384]{1,0:T(8,128)}, u32[]{:S(2)}) copy-start(f32[256,384]{1,0:T(8,128)} %param.30) | copy-start | bytes 1179652
  634.7 481.6 %all-reduce.3.cloned.1.call-start = ((), (), s32[]{:S(2)}) async-start(), calls=%async_computation.15 | async-start | bytes 18350080 | tf_op jit(solution)/shard_map/psum | solution.py:200
  897.4 0.9 copy-start.27
  906.2 7.9 copy-start.43
  906.2 7.9 copy-start.21
  906.2 33.7 %copy-start.38 = (f32[256]{0:T(256)S(1)}, f32[256]{0:T(256)}, u32[]{:S(2)}) copy-start(f32[256]{0:T(256)} %param.37) | copy-start | bytes 3076
  906.2 33.7 %copy-start.39 = (f32[256]{0:T(256)S(1)}, f32[256]{0:T(256)}, u32[]{:S(2)}) copy-start(f32[256]{0:T(256)} %param.45) | copy-start | bytes 3076
  906.2 33.7 %copy-start.40 = (f32[256]{0:T(256)S(1)}, f32[256]{0:T(256)}, u32[]{:S(2)}) copy-start(f32[256]{0:T(256)} %param.53) | copy-start | bytes 3076
  906.2 33.7 %copy-start.41 = (f32[256]{0:T(256)S(1)}, f32[256]{0:T(256)}, u32[]{:S(2)}) copy-start(f32[256]{0:T(256)} %param.52) | copy-start | bytes 3076
  906.2 33.7 %copy-start.42 = (f32[256]{0:T(256)S(1)}, f32[256]{0:T(256)}, u32[]{:S(2)}) copy-start(f32[256]{0:T(256)} %param.44) | copy-start | bytes 3076
  906.2 34.3 %copy-start.34 = (f32[3,256]{1,0:T(4,128)S(1)}, f32[3,256]{1,0:T(4,128)}, u32[]{:S(2)}) copy-start(f32[3,256]{1,0:T(4,128)} %param.43) | copy-start | bytes 9220
  906.2 34.2 %copy-start.35 = (f32[3,256]{1,0:T(4,128)S(1)}, f32[3,256]{1,0:T(4,128)}, u32[]{:S(2)}) copy-start(f32[3,256]{1,0:T(4,128)} %param.51) | copy-start | bytes 9220
  939.8 185.2 %copy-start.32 = (f32[256,1]{0,1:T(1,128)}, f32[256,1]{0,1:T(1,128)S(1)}, u32[]{:S(2)}) copy-start(f32[256,1]{0,1:T(1,128)S(1)} %get-tuple-element.218) | copy-start | bytes 3076
  939.8 185.2 %copy-start.33 = (f32[256,1]{0,1:T(1,128)}, f32[256,1]{0,1:T(1,128)S(1)}, u32[]{:S(2)}) copy-start(f32[256,1]{0,1:T(1,128)S(1)} %get-tuple-element.219) | copy-start | bytes 3076
  1116.3 4.2 copy-start
  1142.0 4.5 copy-start.19
  1142.0 4.5 copy-start.20
  1147.6 15.9 %copy-start.12 = (f32[256,576]{0,1:T(8,128)S(1)}, f32[256,576]{0,1:T(8,128)}, u32[]{:S(2)}) copy-start(f32[256,576]{0,1:T(8,128)} %param.32) | copy-start | bytes 1769476
  1147.6 15.9 %copy-start.13 = (f32[256,576]{0,1:T(8,128)S(1)}, f32[256,576]{0,1:T(8,128)}, u32[]{:S(2)}) copy-start(f32[256,576]{0,1:T(8,128)} %param.33) | copy-start | bytes 1769476
  1147.6 15.9 %copy-start.22 = (f32[256,576]{0,1:T(8,128)S(1)}, f32[256,576]{0,1:T(8,128)}, u32[]{:S(2)}) copy-start(f32[256,576]{0,1:T(8,128)} %param.41) | copy-start | bytes 1769476
  1147.6 15.9 %copy-start.23 = (f32[256,576]{0,1:T(8,128)S(1)}, f32[256,576]{0,1:T(8,128)}, u32[]{:S(2)}) copy-start(f32[256,576]{0,1:T(8,128)} %param.49) | copy-start | bytes 1769476
  1147.6 15.9 %copy-start.24 = (f32[256,576]{0,1:T(8,128)S(1)}, f32[256,576]{0,1:T(8,128)}, u32[]{:S(2)}) copy-start(f32[256,576]{0,1:T(8,128)} %param.48) | copy-start | bytes 1769476
  1147.6 15.9 %copy-start.25 = (f32[256,576]{0,1:T(8,128)S(1)}, f32[256,576]{0,1:T(8,128)}, u32[]{:S(2)}) copy-start(f32[256,576]{0,1:T(8,128)} %param.40) | copy-start | bytes 1769476
Sparse Core Ops, SparseCore 0:
  10.2 27.7 all-gather.11
  40.2 31.7 all-gather.17
  74.3 30.3 all-gather.21
  106.7 31.9 all-gather.25
  140.3 68.7 all-gather.13
  210.9 35.1 all-gather.15
  247.9 96.0 all-gather.19
  345.8 96.0 all-gather.23
  443.8 96.1 all-gather.27
  560.4 95.0 reduce-scatter.5
  658.6 238.7 reduce-scatter.3
  900.5 22.8 reduce-scatter.7
  925.9 190.4 all-reduce.2
where the time goes:
time: 1170 us
  waiting for transfers between devices  895 us (76%)
  matrix products  93.1 us (8%)
  other arithmetic  59.4 us (5%)
  blocking collectives  56 us (5%)
  local copies, waits for them, and re-layouts  49.4 us (4%)
  between operations  14.6 us (1%)
    reduce_scatter x1, waiting for transfers between devices, local(): lax.psum_scatter(wide_terms.astype(jnp.bfloat16), 'own', scatter_dimensio...  242 us
    psum x1, waiting for transfers between devices, local(): lax.psum(shares[0].astype(jnp.bfloat16), 'grp').astype(jnp.float32)  175 us
    all_gather x1, waiting for transfers between devices, local(): lax.all_gather(across[2], 'own', axis=0, tiled=True)  95.3 us
    all_gather x1, waiting for transfers between devices, local(): lax.all_gather(across[4], 'own', axis=0, tiled=True)  86.5 us
    all_gather x1, waiting for transfers between devices, local(): lax.all_gather(across[3], 'own', axis=0, tiled=True)  86.4 us
    all_gather x1, waiting for transfers between devices, local(): lax.all_gather(across[0], 'own', axis=0, tiled=True)  53.3 us
    unnamed x106, local copies, waits for them, and re-layouts  40 us
    all_gather x1, waiting for transfers between devices, local(): lax.all_gather(w_down.astype(jnp.bfloat16), 'grp', axis=1, tiled=True)  33.9 us
  transfers between devices with their start and end apart: 15, of which 13 were waited for; matrix products, arithmetic and copies ran while one was open for 11% of the time, Pallas kernels for 0%

commit v1 on v0

--- a/solution.py
+++ b/solution.py
@@ -197,7 +197,7 @@
         ).astype(jnp.float32),
     )
     wide_share, down_share, small_share = (
-        lax.psum(shares[0].astype(jnp.bfloat16), "grp").astype(jnp.float32),
+        jnp.sum(lax.all_gather(shares[0].astype(jnp.bfloat16), "grp"), axis=0).astype(jnp.float32),
         lax.psum(shares[1].astype(jnp.bfloat16), "grp").astype(jnp.float32),
         lax.psum(shares[2].astype(jnp.bfloat16), "grp").astype(jnp.float32),
     )

time: 1170 us -> 1510 us (1.29)
  waiting for transfers between devices: 895 us -> 1240 us
  local copies, waits for them, and re-layouts: 49.4 us -> 27.1 us
    all_gather x0 -> x1, waiting for transfers between devices: none -> 456 us  [local(): lax.all_gather(shares[0].astype(jnp.bfloat16), 'grp')]
    psum x1, waiting for transfers between devices: 175 us -> 51.7 us  [local(): lax.psum(shares[1].astype(jnp.bfloat16), 'grp').astype(jnp.float32)]
    unnamed x106, local copies, waits for them, and re-layouts: 40 us -> 13.6 us
    reduce_sum x0 -> x1, other arithmetic: none -> 21.7 us  [local(): jnp.sum(lax.all_gather(shares[0].astype(jnp.bfloat16), 'grp'), axis=0)]
  transfers between devices with their start and end apart: 15 -> 16, of which waited for: 13 -> 14; matrix products, arithmetic and copies ran while one was open for 11% -> 8% of each run, Pallas kernels for 0% -> 0%
where the time goes in v1:
time: 1510 us
  waiting for transfers between devices  1240 us (82%)
  matrix products  89.8 us (6%)
  other arithmetic  71.7 us (5%)
  blocking collectives  56.2 us (4%)
  local copies, waits for them, and re-layouts  27.1 us (2%)
    all_gather x1, waiting for transfers between devices, local(): lax.all_gather(shares[0].astype(jnp.bfloat16), 'grp')  456 us
    reduce_scatter x1, waiting for transfers between devices, local(): lax.psum_scatter(wide_terms.astype(jnp.bfloat16), 'own', scatter_dimensio...  242 us
    all_gather x1, waiting for transfers between devices, local(): lax.all_gather(across[2], 'own', axis=0, tiled=True)  95.3 us
    all_gather x1, waiting for transfers between devices, local(): lax.all_gather(across[4], 'own', axis=0, tiled=True)  86.5 us
    all_gather x1, waiting for transfers between devices, local(): lax.all_gather(across[3], 'own', axis=0, tiled=True)  86.5 us
    all_gather x1, waiting for transfers between devices, local(): lax.all_gather(across[0], 'own', axis=0, tiled=True)  53.3 us
    psum x1, waiting for transfers between devices, local(): lax.psum(shares[1].astype(jnp.bfloat16), 'grp').astype(jnp.float32)  51.7 us
    all_gather x1, waiting for transfers between devices, local(): lax.all_gather(w_down.astype(jnp.bfloat16), 'grp', axis=1, tiled=True)  33.9 us
  transfers between devices with their start and end apart: 16, of which 14 were waited for; matrix products, arithmetic and copies ran while one was open for 8% of the time, Pallas kernels for 0%

profile of v1, /device:TPU:0, one launch (start us, length us, event | category | flops | bytes accessed | tf_op | source)
XLA Modules:
  0.0 1506.1 jit_solution(1219529569255696316)
XLA Ops:
  7.3 1.7 convert_element_type.93
  9.1 1.8 convert_element_type.101
  11.0 1.8 convert_element_type.102
  12.8 1.8 convert_element_type.104
  14.7 23.3 %all-gather.14.cloned.1.call-done = bf16[256,3072]{1,0:T(8,128)(2,1)} async-done(((bf16[256,384]{1,0:T(8,128)(2,1)}), bf16[256,3072]{1,0:T(8,128)(2,1)}) %all-gather.14.cloned.1.call-update) | async-done | bytes 1572880 | tf_op jit(solution)/shard_map/all_gather | solution.py:74
  38.1 14.9 all_gather.49
  53.1 18.9 %all-gather.20.cloned.1.call-done = bf16[256,4608]{0,1:T(8,128)(2,1)} async-done(((bf16[256,576]{0,1:T(8,128)(2,1)}), bf16[256,4608]{0,1:T(8,128)(2,1)}) %all-gather.20.cloned.1.call-update) | async-done | bytes 2359312 | tf_op jit(solution)/shard_map/all_gather | solution.py:76
  72.1 32.5 %all-gather.24.cloned.1.call-done = bf16[256,4608]{0,1:T(8,128)(2,1)} async-done(((bf16[256,576]{0,1:T(8,128)(2,1)}), bf16[256,4608]{0,1:T(8,128)(2,1)}) %all-gather.24.cloned.1.call-update) | async-done | bytes 2359312 | tf_op jit(solution)/shard_map/all_gather | solution.py:77
  104.7 33.9 %all-gather.28.cloned.1.call-done = bf16[1152,1024]{1,0:T(8,128)(2,1)} async-done(((bf16[1152,128]{1,0:T(8,128)(2,1)}), bf16[1152,1024]{1,0:T(8,128)(2,1)}) %all-gather.28.cloned.1.call-update) | async-done | bytes 2359312 | tf_op jit(solution)/shard_map/all_gather | solution.py:78
  138.7 8.0 all-gather.1
  147.2 8.3 all_gather.48
  155.9 53.3 %all-gather.16.cloned.1.call-done = bf16[1024,3072]{1,0:T(8,128)(2,1)} async-done(((bf16[256,3072]{1,0:T(8,128)(2,1)}), bf16[1024,3072]{1,0:T(8,128)(2,1)}) %all-gather.16.cloned.1.call-update) | async-done | bytes 6291472 | tf_op jit(solution)/shard_map/all_gather | solution.py:81
  209.2 4.7 fusion.30
  214.0 3.4 collective-permute-start
  217.5 8.7 all-gather.2
  226.2 1.5 multiply_convert_fusion.7
  227.7 18.4 %all-gather.18.cloned.1.call-done = bf16[1024,1024]{1,0:T(8,128)(2,1)} async-done(((bf16[256,1024]{1,0:T(8,128)(2,1)}), bf16[1024,1024]{1,0:T(8,128)(2,1)}) %all-gather.18.cloned.1.call-update) | async-done | bytes 2097168 | tf_op jit(solution)/shard_map/all_gather | solution.py:82
  246.1 2.4 multiply_reduce_fusion.2
  248.7 95.3 %all-gather.22.cloned.1.call-done = bf16[1024,4608]{0,1:T(8,128)(2,1)} async-done(((bf16[256,4608]{0,1:T(8,128)(2,1)}), bf16[1024,4608]{0,1:T(8,128)(2,1)}) %all-gather.22.cloned.1.call-update) | async-done | bytes 9437200 | tf_op jit(solution)/shard_map/all_gather | solution.py:83
  344.0 11.5 fusion.51
  355.5 86.5 %all-gather.26.cloned.1.call-done = bf16[1024,4608]{0,1:T(8,128)(2,1)} async-done(((bf16[256,4608]{0,1:T(8,128)(2,1)}), bf16[1024,4608]{0,1:T(8,128)(2,1)}) %all-gather.26.cloned.1.call-update) | async-done | bytes 9437200 | tf_op jit(solution)/shard_map/all_gather | solution.py:84
  441.9 11.5 fusion.52
  453.5 86.5 %all-gather.30.cloned.1.call-done = bf16[4608,1024]{1,0:T(8,128)(2,1)} async-done(((bf16[1152,1024]{1,0:T(8,128)(2,1)}), bf16[4608,1024]{1,0:T(8,128)(2,1)}) %all-gather.30.cloned.1.call-update) | async-done | bytes 9437200 | tf_op jit(solution)/shard_map/all_gather | solution.py:85
  540.0 13.8 multiply_convert_fusion
  553.8 1.4 copy-done.15
  555.2 5.1 convolution_convert_fusion
  560.6 6.0 fusion.53
  567.0 2.0 slice-done.2
  569.0 3.0 multiply_reduce_fusion
  573.2 2.7 select_reduce_fusion
  576.0 1.0 copy-done.13
  576.9 1.5 collective-permute-start.1
  578.5 5.2 convolution_convert_fusion.1
  583.7 5.2 convolution_convert_fusion.2
  588.8 2.1 convolution_convert_fusion.4
  590.9 4.1 copy.67
  595.0 3.1 multiply_convert_fusion.5
  598.1 1.6 multiply_convert_fusion.3
  599.7 4.7 convolution_convert_fusion.3
  604.4 18.8 %pad_maximum_fusion = bf16[1024,13312]{1,0:T(8,128)(2,1)} fusion(bf16[1024,4608]{1,0:T(8,128)(2,1)} %convolution_convert_fusion.1, bf16[1024,4608]{1,0:T(8,128)(2,1)} %convolution_convert_fusion.2, bf16[1024,1024]{1,0:T(8,128)(2,1)S(1)} %copy-done.3, bf16[1024,3072]{1,0:T(8,128)(2,1)} %convolution_convert_fusion.3), kind=kLoop, calls=%fused_computation | loop fusion | flops 109051904 | bytes 54525952 | tf_op jit(solution)/shard_map/concatenate | solution.py:178
  623.5 6.1 fusion.18
  630.4 25.2 %reduce-scatter.6.cloned.1.call-done = bf16[1152,1024]{1,0:T(8,128)(2,1)} async-done(((bf16[4608,1024]{1,0:T(8,128)(2,1)}), bf16[1152,1024]{1,0:T(8,128)(2,1)}) %reduce-scatter.6.cloned.1.call-update) | async-done | bytes 2359312 | tf_op jit(solution)/shard_map/reduce_scatter | solution.py:192
  655.6 241.8 %reduce-scatter.4.cloned.1.call-done = bf16[256,13312]{1,0:T(8,128)(2,1)} async-done(((bf16[1024,13312]{1,0:T(8,128)(2,1)}), bf16[256,13312]{1,0:T(8,128)(2,1)}) %reduce-scatter.4.cloned.1.call-update) | async-done | bytes 6815760 | tf_op jit(solution)/shard_map/reduce_scatter | solution.py:189
  897.5 7.9 fusion.1
  905.4 1.2 fusion.14
  906.6 16.9 %reduce-scatter.8.cloned.1.call-done = bf16[256,5]{0,1:T(8,128)(2,1)} async-done(((bf16[1024,5]{0,1:T(8,128)(2,1)}), bf16[256,5]{0,1:T(8,128)(2,1)}) %reduce-scatter.8.cloned.1.call-update) | async-done | bytes 2576 | tf_op jit(solution)/shard_map/reduce_scatter | solution.py:195
  923.5 16.2 %psum.15 = bf16[256,5]{0,1:T(8,128)(2,1)S(1)} all-reduce(bf16[256,5]{0,1:T(8,128)(2,1)} %reduce-scatter.8.cloned.1.call-done), channel_id=1, replica_groups=mesh['grp'=8,'own'=4] {'grp'}, use_global_device_ids=true, to_apply=%region_16.17 | all-reduce | flops 1280 | bytes 5120 | tf_op jit(solution)/shard_map/psum | solution.py:202
  941.0 51.7 %all-reduce.2.cloned.1.call-done = bf16[1152,1024]{1,0:T(8,128)(2,1)} async-done(((bf16[1152,1024]{1,0:T(8,128)(2,1)}), bf16[1152,1024]{1,0:T(8,128)(2,1)}) %all-reduce.2.cloned.1.call-update) | async-done | bytes 2359312 | tf_op jit(solution)/shard_map/psum | solution.py:201
  992.7 2.2 convert_element_type.113
  994.9 2.2 copy-done.6
  997.1 1.5 multiply_subtract_fusion.1
  998.6 456.1 %all-gather.32.cloned.1.call-done = bf16[2048,13312]{1,0:T(8,128)(2,1)} async-done(((bf16[256,13312]{1,0:T(8,128)(2,1)}), bf16[2048,13312]{1,0:T(8,128)(2,1)}) %all-gather.32.cloned.1.call-update) | async-done | bytes 54525968 | tf_op jit(solution)/shard_map/all_gather | solution.py:200
  1454.7 21.7 %reduce_sum.97 = bf16[256,13312]{1,0:T(8,128)(2,1)} reduce(bf16[8,256,13312]{2,1,0:T(8,128)(2,1)} %bitcast.35, bf16[]{:T(256)} %constant.43.clone.1), dimensions={0}, to_apply=%region_7.8 | reduce | flops 23855104 | bytes 61341696 | tf_op jit(solution)/shard_map/reduce_sum | solution.py:200
  1476.4 1.9 slice.111
  1478.4 3.7 slice.112
  1482.0 1.2 fusion.48
  1483.3 2.2 copy-done.4
  1485.4 1.9 constant_dynamic-slice_fusion
  1487.3 2.1 copy.70
  1489.4 2.1 copy.71
  1491.6 1.9 multiply_subtract_fusion.5
  1493.5 3.1 multiply_subtract_fusion.3
  1496.6 1.5 multiply_subtract_fusion.2
  1498.1 1.2 multiply_subtract_fusion.4
  (167 shorter events, 6.0 us)
Async XLA Ops:
  7.2 30.9 %copy-start.30 = (f32[256,128]{1,0:T(8,128)S(1)}, f32[256,128]{1,0:T(8,128)}, u32[]{:S(2)}) copy-start(f32[256,128]{1,0:T(8,128)} %param.31) | copy-start | bytes 393220
  7.2 30.8 %all-gather.14.cloned.1.call-start = ((), (), s32[]{:S(2)}) async-start(), calls=%async_computation.3 | async-start | bytes 1769472 | tf_op jit(solution)/shard_map/all_gather | solution.py:74
  9.0 63.0 %all-gather.20.cloned.1.call-start = ((), (), s32[]{:S(2)}) async-start(), calls=%async_computation.6 | async-start | bytes 2654208 | tf_op jit(solution)/shard_map/all_gather | solution.py:76
  10.9 93.7 %all-gather.24.cloned.1.call-start = ((), (), s32[]{:S(2)}) async-start(), calls=%async_computation.8 | async-start | bytes 2654208 | tf_op jit(solution)/shard_map/all_gather | solution.py:77
  12.8 125.8 %all-gather.28.cloned.1.call-start = ((), (), s32[]{:S(2)}) async-start(), calls=%async_computation.10 | async-start | bytes 2654208 | tf_op jit(solution)/shard_map/all_gather | solution.py:78
  14.7 194.5 %all-gather.16.cloned.1.call-start = ((), (), s32[]{:S(2)}) async-start(), calls=%async_computation.4 | async-start | bytes 7864320 | tf_op jit(solution)/shard_map/all_gather | solution.py:81
  38.0 100.7 %copy-start.42 = (f32[256]{0:T(256)S(1)}, f32[256]{0:T(256)}, u32[]{:S(2)}) copy-start(f32[256]{0:T(256)} %param.36) | copy-start | bytes 3076
  38.0 108.8 %copy-start.36 = (f32[3,256]{1,0:T(4,128)S(1)}, f32[3,256]{1,0:T(4,128)}, u32[]{:S(2)}) copy-start(f32[3,256]{1,0:T(4,128)} %param.35) | copy-start | bytes 9220
  38.0 108.8 %copy-start.37 = (s32[4,4]{1,0:T(4,128)S(1)}, s32[4,4]{1,0:T(4,128)}, u32[]{:S(2)}) copy-start(s32[4,4]{1,0:T(4,128)} %param.29) | copy-start | bytes 196
  38.0 117.6 %copy-start.9 = (bf16[256,1024]{1,0:T(8,128)(2,1)S(1)}, bf16[256,1024]{1,0:T(8,128)(2,1)}, u32[]{:S(2)}) copy-start(bf16[256,1024]{1,0:T(8,128)(2,1)} %param.27) | copy-start | bytes 1572868
  38.1 208.0 %all-gather.18.cloned.1.call-start = ((), (), s32[]{:S(2)}) async-start(), calls=%async_computation.5 | async-start | bytes 2621440 | tf_op jit(solution)/shard_map/all_gather | solution.py:82
  53.0 291.0 %all-gather.22.cloned.1.call-start = ((), (), s32[]{:S(2)}) async-start(), calls=%async_computation.7 | async-start | bytes 11796480 | tf_op jit(solution)/shard_map/all_gather | solution.py:83
  72.1 369.9 %all-gather.26.cloned.1.call-start = ((), (), s32[]{:S(2)}) async-start(), calls=%async_computation.9 | async-start | bytes 11796480 | tf_op jit(solution)/shard_map/all_gather | solution.py:84
  104.7 435.4 %all-gather.30.cloned.1.call-start = ((), (), s32[]{:S(2)}) async-start(), calls=%async_computation.11 | async-start | bytes 11796480 | tf_op jit(solution)/shard_map/all_gather | solution.py:85
  138.7 516.9 %reduce-scatter.6.cloned.1.call-start = ((), (), s32[]{:S(2)}) async-start(), calls=%async_computation.13 | async-start | bytes 11796480 | tf_op jit(solution)/shard_map/reduce_scatter | solution.py:192
  209.2 8.3 copy-start.43
  213.8 12.3 copy-start.1
  214.0 12.2 collective-permute-start
  227.7 127.8 %copy-start.11 = (bf16[256,1024]{1,0:T(8,128)(2,1)}, bf16[256,1024]{1,0:T(8,128)(2,1)S(1)}, u32[]{:S(2)}) copy-start(bf16[256,1024]{1,0:T(8,128)(2,1)S(1)} %get-tuple-element.69) | copy-start | bytes 1572868
  248.7 193.3 %copy-start.7 = (bf16[256,1024]{1,0:T(8,128)(2,1)}, bf16[256,1024]{1,0:T(8,128)(2,1)S(1)}, u32[]{:S(2)}) copy-start(bf16[256,1024]{1,0:T(8,128)(2,1)S(1)} %multiply_convert_fusion.6) | copy-start | bytes 1572868
  441.9 98.1 %copy-start.22 = (bf16[256,1024]{1,0:T(8,128)(2,1)S(1)}, bf16[256,1024]{1,0:T(8,128)(2,1)}, u32[]{:S(2)}) copy-start(bf16[256,1024]{1,0:T(8,128)(2,1)} %param.28) | copy-start | bytes 1572868
  560.3 6.3 slice-start
  560.3 337.1 %reduce-scatter.4.cloned.1.call-start = ((), (), s32[]{:S(2)}) async-start(), calls=%async_computation.12 | async-start | bytes 34078720 | tf_op jit(solution)/shard_map/reduce_scatter | solution.py:189
  560.5 6.1 copy-start.21
  560.5 6.5 slice-start.1
  560.6 8.4 slice-start.2
  569.0 3.0 copy-start.23
  569.0 3.4 copy-start.2
  572.4 6.1 copy-start.8
  576.9 6.7 copy-start.20
  576.9 18.1 %collective-permute-start.1 = (f32[2,1024]{1,0:T(2,128)S(1)}, f32[2,1024]{1,0:T(2,128)S(1)}, u32[]{:S(2)}, u32[]{:S(2)}) collective-permute-start(f32[2,1024]{1,0:T(2,128)S(1)} %slice.108), channel_id=1, source_target_pairs={{1,0},{2,1},{3,2},{4,3},{5,4},{6,5},{7,6},{8,7},{9,8},{10,9},{11,1... | collective-permute-start | bytes 24584 | tf_op jit(solution)/shard_map/ppermute | solution.py:20
  583.7 5.2 copy-start.12
  590.9 8.8 copy-start.10
  595.0 4.7 copy-start.31
  598.1 6.3 copy-start.32
  599.7 4.7 copy-start.3
  623.2 300.2 %reduce-scatter.8.cloned.1.call-start = ((), (), s32[]{:S(2)}) async-start(), calls=%async_computation.15 | async-start | bytes 20480 | tf_op jit(solution)/shard_map/reduce_scatter | solution.py:195
  630.3 362.4 %all-reduce.2.cloned.1.call-start = ((), (), s32[]{:S(2)}) async-start(), calls=%async_computation.14 | async-start | bytes 4718592 | tf_op jit(solution)/shard_map/psum | solution.py:201
  655.6 799.1 %all-gather.32.cloned.1.call-start = ((), (), s32[]{:S(2)}) async-start(), calls=%async_computation.16 | async-start | bytes 61341696 | tf_op jit(solution)/shard_map/all_gather | solution.py:200
  897.4 7.9 copy-start.25
  897.4 42.3 %copy-start.44 = (f32[256]{0:T(256)S(1)}, f32[256]{0:T(256)}, u32[]{:S(2)}) copy-start(f32[256]{0:T(256)} %param.45) | copy-start | bytes 3076
  897.5 42.3 %copy-start.45 = (f32[256]{0:T(256)S(1)}, f32[256]{0:T(256)}, u32[]{:S(2)}) copy-start(f32[256]{0:T(256)} %param.53) | copy-start | bytes 3076
  897.5 42.3 %copy-start.46 = (f32[256]{0:T(256)S(1)}, f32[256]{0:T(256)}, u32[]{:S(2)}) copy-start(f32[256]{0:T(256)} %param.52) | copy-start | bytes 3076
  897.5 42.3 %copy-start.47 = (f32[256]{0:T(256)S(1)}, f32[256]{0:T(256)}, u32[]{:S(2)}) copy-start(f32[256]{0:T(256)} %param.44) | copy-start | bytes 3076
  897.5 42.9 %copy-start.40 = (f32[3,256]{1,0:T(4,128)S(1)}, f32[3,256]{1,0:T(4,128)}, u32[]{:S(2)}) copy-start(f32[3,256]{1,0:T(4,128)} %param.43) | copy-start | bytes 9220
  897.5 42.9 %copy-start.41 = (f32[3,256]{1,0:T(4,128)S(1)}, f32[3,256]{1,0:T(4,128)}, u32[]{:S(2)}) copy-start(f32[3,256]{1,0:T(4,128)} %param.51) | copy-start | bytes 9220
  905.4 91.7 %copy-start.17 = (f32[1152,128]{1,0:T(8,128)S(1)}, f32[1152,128]{1,0:T(8,128)}, u32[]{:S(2)}) copy-start(f32[1152,128]{1,0:T(8,128)} %param.34) | copy-start | bytes 1769476
  905.4 91.7 %copy-start.26 = (f32[1152,128]{1,0:T(8,128)S(1)}, f32[1152,128]{1,0:T(8,128)}, u32[]{:S(2)}) copy-start(f32[1152,128]{1,0:T(8,128)} %param.42) | copy-start | bytes 1769476
  905.4 91.7 %copy-start.27 = (f32[1152,128]{1,0:T(8,128)S(1)}, f32[1152,128]{1,0:T(8,128)}, u32[]{:S(2)}) copy-start(f32[1152,128]{1,0:T(8,128)} %param.50) | copy-start | bytes 1769476
  939.7 58.9 %copy-start.38 = (f32[256,1]{0,1:T(1,128)}, f32[256,1]{0,1:T(1,128)S(1)}, u32[]{:S(2)}) copy-start(f32[256,1]{0,1:T(1,128)S(1)} %get-tuple-element.80) | copy-start | bytes 3076
  939.7 58.9 %copy-start.39 = (f32[256,1]{0,1:T(1,128)}, f32[256,1]{0,1:T(1,128)S(1)}, u32[]{:S(2)}) copy-start(f32[256,1]{0,1:T(1,128)S(1)} %get-tuple-element.81) | copy-start | bytes 3076
  994.9 2.2 copy-start.6
  1476.4 5.6 copy-start
  1478.4 19.8 %copy-start.16 = (f32[256,3072]{1,0:T(8,128)}, f32[256,3072]{1,0:T(8,128)S(1)}, u32[]{:S(2)}) copy-start(f32[256,3072]{1,0:T(8,128)S(1)} %slice.111) | copy-start | bytes 9437188
  1483.3 2.2 copy-start.4
  1483.3 4.0 copy-start.5
  1483.3 8.3 copy-start.35
  1491.5 5.1 copy-start.18
  1491.5 5.1 copy-start.19
  1491.6 5.1 copy-start.28
  1491.6 5.1 copy-start.29
  1491.6 6.6 copy-start.24
  1491.6 6.5 copy-start.33
  1491.6 6.5 copy-start.34
  (3 other events, 3.6 us)
Sparse Core Ops, SparseCore 0:
  10.2 27.7 all-gather.13
  40.2 31.7 all-gather.19
  74.3 30.3 all-gather.23
  106.7 31.9 all-gather.27
  140.3 68.7 all-gather.15
  210.9 35.1 all-gather.17
  247.9 96.0 all-gather.21
  345.8 96.0 all-gather.25
  443.8 96.1 all-gather.29
  560.4 95.0 reduce-scatter.5
  658.7 238.6 reduce-scatter.3
  900.6 22.8 reduce-scatter.7
  925.8 66.8 all-reduce.1
  994.2 460.4 all-gather.31
